TPU v7x, 256 devices: a whole 4x4x8 slice. The times are simulated.
256 devices in a mesh: sky: 32 (over z_lo, y, core), edge: 8 (over x, z_hi).
Axes of the slice: x: 4, y: 4, z: 8 (z_hi: 2, z_lo: 4; z = z_hi * 4 + z_lo), core: 2. Of those that a mesh axis runs over, the one named last changes fastest.
Arguments:
- node_feats: bfloat16 [131072, 128], P('sky'), may hold values from -6 to 6
- saved_agg: bfloat16 [131072, 128], P('sky'), may hold values from -9 to 9
- node_cot: bfloat16 [131072, 128], P('sky'), may hold values from -6 to 6
- edge_feats: bfloat16 [2097152, 128], P(('sky', 'edge')), may hold values from -6 to 6
- edge_cot: bfloat16 [2097152, 128], P(('sky', 'edge')), may hold values from -6 to 6
- senders: int32 [2097152], P(('sky', 'edge')), may hold values from 0 to 8191, as said below
- counts: int32 [131072], P('sky'), may hold values from 0 to 16, as said below
- send_lower: int32 [65536], P('sky'), may hold values from 0 to 4095, as said below
- send_upper: int32 [65536], P('sky'), may hold values from 0 to 4095, as said below
- w_recv: bfloat16 [128, 128], replicated, may hold values from -0.3125 to 0.3125
- w_send: bfloat16 [128, 128], replicated, may hold values from -0.3125 to 0.3125
- w_edge: bfloat16 [128, 128], replicated, may hold values from -0.3125 to 0.3125
- w_out: bfloat16 [128, 128], replicated, may hold values from -0.5 to 0.5
- b_edge: float32 [128], replicated, may hold values from -3 to 3
- v_self: bfloat16 [128, 128], replicated, may hold values from -0.375 to 0.375
- v_agg: bfloat16 [128, 128], replicated, may hold values from -0.375 to 0.375
- v_out: bfloat16 [128, 128], replicated, may hold values from -0.5 to 0.5
- b_node: float32 [128], replicated, may hold values from -3 to 3
Outputs:
- node_grad: bfloat16 [131072, 128], P('sky')
- edge_grad: bfloat16 [2097152, 128], P(('sky', 'edge'))
- edge_weight_grads: float32 [4, 128, 128], replicated
- node_weight_grads: float32 [3, 128, 128], replicated
- bias_grads: float32 [2, 128], replicated
Inputs may be any that keep to these rules, and one draw needn't show every extreme that they name: `senders`: A sender below 4096 is a node of the receiver's own tile; from 4096 up it is a halo slot of halo_rows. Dead slots name a sender too. `counts`: counts differ from tile to tile. `send_lower`: each tile's 2048 entries are distinct node rows of that tile. `send_upper`: each tile's 2048 entries are distinct node rows of that tile.
All inputs are finite; a program needn't handle non-finite values.
Results may differ from a plain program's by a relative error of at most 0.012.
Values may be sent and summed in bfloat16 or wider, within the bound.
A program may use at most 128 MiB of HBM per device.

v0:
```python
import jax
import jax.numpy as jnp
from jax import lax
from jax.sharding import PartitionSpec as P

DEGREE = 16


def passed_along(array, axis, by):
    size = lax.axis_size(axis)
    return lax.ppermute(array, axis, [(i, (i + by) % size) for i in range(size)])


def slope(z):
    s = jax.nn.sigmoid(z)
    return s * (1.0 + z * (1.0 - s))


def matmul(a, b):
    return jnp.dot(a, b, preferred_element_type=jnp.float32)


def outer_sum(a, b):
    return jnp.einsum("ef,eg->fg", a, b, preferred_element_type=jnp.float32)


def shards(
    node_feats,
    saved_agg,
    node_cot,
    edge_feats,
    edge_cot,
    senders,
    counts,
    send_lower,
    send_upper,
    w_recv,
    w_send,
    w_edge,
    w_out,
    b_edge,
    v_self,
    v_agg,
    v_out,
    b_node,
):
    nodes = node_feats.shape[0]
    width = node_feats.shape[1]
    halo = send_lower.shape[0]
    groups = lax.axis_size("edge")
    member = lax.axis_index("edge")
    share = nodes // groups
    start = member * share
    upper_rows = jnp.take(node_feats, send_upper, axis=0)
    lower_rows = jnp.take(node_feats, send_lower, axis=0)
    from_lower = passed_along(upper_rows, "sky", 1)
    from_upper = passed_along(lower_rows, "sky", -1)
    all_rows = jnp.concatenate([node_feats, from_lower, from_upper], axis=0)
    own = lax.dynamic_slice_in_dim(node_feats, start, share, 0)
    own_agg = lax.dynamic_slice_in_dim(saved_agg, start, share, 0)
    own_cot = lax.dynamic_slice_in_dim(node_cot, start, share, 0)
    own_counts = lax.dynamic_slice_in_dim(counts, start, share, 0)
    pre_node = matmul(own, v_self) + matmul(own_agg, v_agg) + b_node
    node_act = jax.nn.silu(pre_node).astype(jnp.bfloat16)
    d_pre_node = (matmul(own_cot, v_out.T) * slope(pre_node)).astype(jnp.bfloat16)
    d_agg = matmul(d_pre_node, v_agg.T).astype(jnp.bfloat16)
    d_node = own_cot.astype(jnp.float32) + matmul(d_pre_node, v_self.T)
    sender_rows = jnp.take(all_rows, senders, axis=0)
    pre_edge = (
        jnp.repeat(matmul(own, w_recv), DEGREE, axis=0)
        + matmul(sender_rows, w_send)
        + matmul(edge_feats, w_edge)
        + b_edge
    )
    hidden = jax.nn.silu(pre_edge).astype(jnp.bfloat16)
    live = (
        (jnp.arange(DEGREE, dtype=jnp.int32)[None, :] < own_counts[:, None])
        .astype(jnp.float32)
        .reshape(-1, 1)
    )
    d_msg = (
        (edge_cot.astype(jnp.float32) + jnp.repeat(d_agg.astype(jnp.float32), DEGREE, axis=0))
        * live
    ).astype(jnp.bfloat16)
    d_pre = (matmul(d_msg, w_out.T) * slope(pre_edge)).astype(jnp.bfloat16)
    edge_grad = matmul(d_pre, w_edge.T).astype(jnp.bfloat16)
    to_recv = matmul(d_pre, w_recv.T).reshape(share, DEGREE, width).sum(axis=1)
    to_send = jax.ops.segment_sum(matmul(d_pre, w_send.T), senders, num_segments=nodes + 2 * halo)
    local = to_send[:nodes]
    cot_lower = to_send[nodes : nodes + halo]
    cot_upper = to_send[nodes + halo :]
    back_upper = passed_along(cot_lower.astype(jnp.bfloat16), "sky", -1).astype(cot_lower.dtype)
    back_lower = passed_along(cot_upper.astype(jnp.bfloat16), "sky", 1).astype(cot_upper.dtype)
    local = local.at[send_upper].add(back_upper).at[send_lower].add(back_lower)
    recv_grad = jnp.einsum(
        "nf,nkg->fg", own, d_pre.reshape(share, DEGREE, width), preferred_element_type=jnp.float32
    )
    bias_terms = jnp.stack(
        [
            jnp.sum(d_pre.astype(jnp.float32), axis=0),
            jnp.sum(d_pre_node.astype(jnp.float32), axis=0),
        ]
    )
    terms = jnp.concatenate(
        [
            recv_grad,
            outer_sum(sender_rows, d_pre),
            outer_sum(edge_feats, d_pre),
            outer_sum(hidden, d_msg),
            outer_sum(own, d_pre_node),
            outer_sum(own_agg, d_pre_node),
            outer_sum(node_act, own_cot),
            bias_terms,
        ],
        axis=0,
    )
    used = terms.shape[0]
    chunk = -(-used // (groups * 8)) * 8
    terms = jnp.pad(terms, ((0, chunk * groups - used), (0, 0)))
    terms = lax.psum(terms, "sky")
    mine = lax.dynamic_slice_in_dim(local, start, share, 0) + d_node + to_recv
    local = lax.dynamic_update_slice_in_dim(local, mine, start, 0)
    summed = lax.psum(jnp.concatenate([local, terms], axis=0), "edge")
    node_grad = summed[:nodes].astype(jnp.bfloat16)
    totals = summed[nodes : nodes + used]
    scale = 1.0 / jnp.sqrt(jnp.float32(lax.axis_size("sky") * nodes * DEGREE))
    totals = totals * scale
    blocks = width
    edge_total = totals[: 4 * blocks].reshape(4, blocks, width)
    node_total = totals[4 * blocks : 7 * blocks].reshape(3, blocks, width)
    bias_total = totals[7 * blocks :]
    return (node_grad, edge_grad, edge_total, node_total, bias_total)


def solution(mesh):
    in_specs = (
        P("sky", None),
        P("sky", None),
        P("sky", None),
        P(("sky", "edge"), None),
        P(("sky", "edge"), None),
        P(("sky", "edge")),
        P("sky"),
        P("sky"),
        P("sky"),
        P(),
        P(),
        P(),
        P(),
        P(),
        P(),
        P(),
        P(),
        P(),
    )
    out_specs = (P("sky", None), P(("sky", "edge"), None), P(), P(), P())
    return jax.shard_map(shards, mesh=mesh, in_specs=in_specs, out_specs=out_specs, check_vma=False)
```

profile of v0, /device:TPU:1, one launch (start us, length us, event | category | flops | bytes accessed | tf_op | source)
XLA Modules:
  0.0 690.7 jit_solution(3772573964208403021)
XLA Ops:
  7.2 0.8 compare_select_fusion.1
  8.8 9.2 %gather_fusion.2 = bf16[2048,128]{1,0:T(8,128)(2,1)} fusion(bf16[4096,128]{1,0:T(8,128)(2,1)} %param.20, s32[2048]{0:T(1024)S(1)} %get-tuple-element.9), kind=kCustom, calls=%fused_computation.1.clone | custom fusion | bytes 1056768 | tf_op jit(solution)/shard_map/jit(_take)/gather | solution.py:55
  17.9 2.2 broadcast_select_fusion.3
  20.1 3.2 collective-permute-start.1
  24.0 8.1 %gather_fusion.1 = bf16[2048,128]{1,0:T(8,128)(2,1)} fusion(bf16[4096,128]{1,0:T(8,128)(2,1)S(1)} %copy-done.1, s32[2048]{0:T(1024)S(1)} %get-tuple-element.11), kind=kCustom, calls=%fused_computation.clone | custom fusion | bytes 1056768 | tf_op jit(solution)/shard_map/jit(_take)/gather | solution.py:54
  32.0 2.2 broadcast_select_fusion.4
  34.4 1.1 fusion.7
  35.5 1.8 convert_reduce_fusion.1
  37.3 0.9 fusion.9
  38.2 0.9 fusion.22
  39.1 1.8 fusion.17
  40.8 1.4 fusion.30
  42.2 0.8 dynamic_slice.18
  43.0 0.8 fusion.15
  43.8 0.8 compare_and_fusion
  44.6 1.7 reshape.64
  46.3 3.5 fusion.3
  50.0 1.8 fusion.16
  51.8 2.7 pad_maximum_fusion.1
  54.5 32.8 %gather_fusion = bf16[8192,128]{1,0:T(8,128)(2,1)} fusion(bf16[8192,128]{1,0:T(8,128)(2,1)} %pad_maximum_fusion.1, s32[8192]{0:T(1024)} %fusion.30), kind=kCustom, calls=%fused_computation.2 | custom fusion | bytes 4227072 | tf_op jit(solution)/shard_map/jit(_take)/gather | solution.py:68
  87.5 1.3 copy-done.5
  88.8 2.7 convolution_add_fusion.1
  92.2 0.9 copy-done.6
  93.1 2.9 bitcast_reduce_fusion
  96.1 2.6 fusion.14
  98.7 0.8 convolution_bitcast_fusion
  99.5 1.9 fusion.6
  101.4 2.7 fusion.44
  104.1 46.5 %scatter_custom_fusion = f32[8192,128]{1,0:T(8,128)} fusion(s32[8192]{0:T(1024)} %param.25, f32[8192,128]{1,0:T(8,128)} %fusion.44, f32[]{:T(128)} %constant.10.clone.1), kind=kCustom, calls=%fused_computation.22 | custom fusion | flops 1048576 | bytes 4194816 | tf_op jit(solution)/shard_map/scatter-add | solution.py:88
  150.5 2.4 convert.9
  153.0 1.1 fusion.43
  154.1 4.8 collective-permute-start.2
  158.9 1.1 convert_reduce_fusion
  160.2 2.6 concatenate.10
  162.8 0.8 pad.4
  163.7 3.2 slice.41
  166.9 0.7 bitcast_reduce_fusion.1
  167.7 13.6 %scatter_custom_fusion.1 = f32[4096,128]{1,0:T(8,128)} fusion(f32[4096,128]{1,0:T(8,128)} %slice.41, s32[2048]{0:T(1024)} %get-tuple-element.10, bf16[2048,128]{1,0:T(8,128)(2,1)} %collective-permute-done.2), kind=kCustom, calls=%fused_computation.37 | custom fusion | flops 524288 | bytes 2621440 | tf_op jit(solution)/shard_map/scatter-add | solution.py:94
  181.3 13.6 %scatter_custom_fusion.2 = f32[4096,128]{1,0:T(8,128)} fusion(f32[4096,128]{1,0:T(8,128)} %scatter_custom_fusion.1, s32[2048]{0:T(1024)S(1)} %get-tuple-element.8, bf16[2048,128]{1,0:T(8,128)(2,1)} %collective-permute-done.3), kind=kCustom, calls=%fused_computation.35 | custom fusion | flops 524288 | bytes 2621440 | tf_op jit(solution)/shard_map/scatter-add | solution.py:94
  194.9 1.9 add_dynamic-update-slice_fusion
  196.8 246.4 %all-reduce.4.cloned.1.call-done = f32[960,128]{1,0:T(8,128)} async-done(((f32[960,128]{1,0:T(8,128)}), f32[960,128]{1,0:T(8,128)}) %all-reduce.4.cloned.1.call-update) | async-done | bytes 491536 | tf_op jit(solution)/shard_map/psum | solution.py:120
  443.2 3.4 pad_maximum_fusion
  446.6 0.7 copy-done.13
  447.4 3.6 convolution_convert_fusion
  451.0 227.2 %all-reduce.6.cloned.1.call-done = f32[5056,128]{1,0:T(8,128)} async-done(((f32[5056,128]{1,0:T(8,128)}), f32[5056,128]{1,0:T(8,128)}) %all-reduce.6.cloned.1.call-update) | async-done | bytes 2588688 | tf_op jit(solution)/shard_map/psum | solution.py:123
  678.2 1.1 slice_multiply_fusion
  679.2 0.7 slice.46
  681.2 2.7 slice.51
  (69 shorter events, 4.3 us)
Async XLA Ops:
  7.2 84.3 %copy-start = (bf16[8192,128]{1,0:T(8,128)(2,1)S(1)}, bf16[8192,128]{1,0:T(8,128)(2,1)}, u32[]{:S(2)}) copy-start(bf16[8192,128]{1,0:T(8,128)(2,1)} %param.23) | copy-start | bytes 6291460
  7.2 436.0 %all-reduce.4.cloned.1.call-start = ((), (), s32[]{:S(2)}) async-start(), calls=%async_computation | async-start | bytes 983040 | tf_op jit(solution)/shard_map/psum | solution.py:120
  8.8 14.5 %copy-start.18 = (s32[2048]{0:T(1024)S(1)}, s32[2048]{0:T(1024)}, u32[]{:S(2)}) copy-start(s32[2048]{0:T(1024)} %param.28) | copy-start | bytes 24580
  8.8 15.2 %copy-start.1 = (bf16[4096,128]{1,0:T(8,128)(2,1)S(1)}, bf16[4096,128]{1,0:T(8,128)(2,1)}, u32[]{:S(2)}) copy-start(bf16[4096,128]{1,0:T(8,128)(2,1)} %param.20) | copy-start | bytes 3145732
  20.1 31.7 %collective-permute-start.1 = (bf16[2048,128]{1,0:T(8,128)(2,1)}, bf16[2048,128]{1,0:T(8,128)(2,1)}, u32[]{:S(2)}, u32[]{:S(2)}) collective-permute-start(bf16[2048,128]{1,0:T(8,128)(2,1)} %broadcast_select_fusion.3), channel_id=1, source_target_pairs={{0,248},{8,0},{16,8},{24,16},{32,24},{40,32},{48,40},{56,48},{64,5... | collective-permute-start | bytes 1572872 | tf_op jit(solution)/shard_map/ppermute | solution.py:11
  23.9 10.3 %copy-start.15 = (bf16[128,128]{1,0:T(8,128)(2,1)S(1)}, bf16[128,128]{1,0:T(8,128)(2,1)}, u32[]{:S(2)}) copy-start(bf16[128,128]{1,0:T(8,128)(2,1)} %param.34) | copy-start | bytes 98308
  23.9 10.4 %copy-start.17 = (bf16[128,128]{1,0:T(8,128)(2,1)S(1)}, bf16[128,128]{1,0:T(8,128)(2,1)}, u32[]{:S(2)}) copy-start(bf16[128,128]{1,0:T(8,128)(2,1)} %param.35) | copy-start | bytes 98308
  24.0 10.4 %copy-start.23 = (f32[128]{0:T(128)S(1)}, f32[128]{0:T(128)}, u32[]{:S(2)}) copy-start(f32[128]{0:T(128)} %param.37) | copy-start | bytes 1540
  32.0 3.5 copy-start.24
  34.2 17.6 %collective-permute-start = (bf16[2048,128]{1,0:T(8,128)(2,1)}, bf16[2048,128]{1,0:T(8,128)(2,1)}, u32[]{:S(2)}, u32[]{:S(2)}) collective-permute-start(bf16[2048,128]{1,0:T(8,128)(2,1)} %broadcast_select_fusion.4), channel_id=1, source_target_pairs={{0,8},{8,16},{16,24},{24,32},{32,40},{40,48},{48,56},{56,64},{64,7... | collective-permute-start | bytes 1572872 | tf_op jit(solution)/shard_map/ppermute | solution.py:11
  35.5 1.8 copy-start.9
  46.3 3.5 copy-start.19
  46.3 3.7 copy-start.10
  87.2 1.6 copy-start.5
  87.2 1.6 copy-start.11
  88.8 2.7 copy-start.12
  88.8 2.7 copy-start.21
  91.5 1.6 copy-start.6
  91.5 1.6 copy-start.25
  96.1 5.3 copy-start.2
  152.9 5.9 copy-start.3
  152.9 7.0 %copy-start.14 = (bf16[512,128]{1,0:T(8,128)(2,1)S(1)}, bf16[512,128]{1,0:T(8,128)(2,1)}, u32[]{:S(2)}) copy-start(bf16[512,128]{1,0:T(8,128)(2,1)} %get-tuple-element.12) | copy-start | bytes 393220
  152.9 7.2 %copy-start.7 = (f32[128,128]{1,0:T(8,128)S(1)}, f32[128,128]{1,0:T(8,128)}, u32[]{:S(2)}) copy-start(f32[128,128]{1,0:T(8,128)} %fusion.22) | copy-start | bytes 196612
  153.0 7.2 %copy-start.8 = (f32[128,128]{1,0:T(8,128)S(1)}, f32[128,128]{1,0:T(8,128)}, u32[]{:S(2)}) copy-start(f32[128,128]{1,0:T(8,128)} %fusion.17) | copy-start | bytes 196612
  153.0 7.2 %copy-start.22 = (f32[128]{0:T(128)S(1)}, f32[128]{0:T(128)}, u32[]{:S(2)}) copy-start(f32[128]{0:T(128)} %get-tuple-element.14) | copy-start | bytes 1540
  154.1 13.6 %collective-permute-start.2 = (bf16[2048,128]{1,0:T(8,128)(2,1)}, bf16[2048,128]{1,0:T(8,128)(2,1)}, u32[]{:S(2)}, u32[]{:S(2)}) collective-permute-start(bf16[2048,128]{1,0:T(8,128)(2,1)} %get-tuple-element.7), channel_id=1, source_target_pairs={{0,248},{8,0},{16,8},{24,16},{32,24},{40,32},{48,40},{56,48},{64,5... | collective-permute-start | bytes 1572872 | tf_op jit(solution)/shard_map/ppermute | solution.py:11
  158.9 22.4 %collective-permute-start.3 = (bf16[2048,128]{1,0:T(8,128)(2,1)}, bf16[2048,128]{1,0:T(8,128)(2,1)}, u32[]{:S(2)}, u32[]{:S(2)}) collective-permute-start(bf16[2048,128]{1,0:T(8,128)(2,1)} %get-tuple-element.6), channel_id=1, source_target_pairs={{0,8},{8,16},{16,24},{24,32},{32,40},{40,48},{48,56},{56,64},{64,7... | collective-permute-start | bytes 1572872 | tf_op jit(solution)/shard_map/ppermute | solution.py:11
  163.7 3.3 copy-start.20
  163.7 514.5 %all-reduce.6.cloned.1.call-start = ((), (), s32[]{:S(2)}) async-start(), calls=%async_computation.1 | async-start | bytes 5177344 | tf_op jit(solution)/shard_map/psum | solution.py:123
  163.7 3.2 copy-start.4
  167.7 27.2 %copy-start.16 = (bf16[128,128]{1,0:T(8,128)(2,1)S(1)}, bf16[128,128]{1,0:T(8,128)(2,1)}, u32[]{:S(2)}) copy-start(bf16[128,128]{1,0:T(8,128)(2,1)} %param.34) | copy-start | bytes 98308
  446.6 0.8 copy-start.13
Sparse Core Ops, SparseCore 0:
  163.8 279.3 all-reduce.3
  446.8 231.3 all-reduce.5
where the time goes:
time: 693 us; the launch traced here: 691 us
  waiting for transfers between devices  474 us (68%)
  other arithmetic  97.3 us (14%)
  local copies, waits for them, and re-layouts  68 us (10%)
  matrix products  29.3 us (4%)
  between operations  14.4 us (2%)
  starting transfers between devices  8.09 us (1%)
    psum x1, waiting for transfers between devices, shards(): terms = lax.psum(terms, 'sky')  246 us
    psum x1, waiting for transfers between devices, shards(): summed = lax.psum(jnp.concatenate([local, terms], axis=0), 'edge')  227 us
    scatter-add x1, other arithmetic, shards(): jax.ops.segment_sum(matmul(d_pre, w_send.T), senders, num_segments=nodes...  46.5 us
    gather x1, local copies, waits for them, and re-layouts, shards(): sender_rows = jnp.take(all_rows, senders, axis=0)  32.8 us
    scatter-add x2, other arithmetic, shards(): local = local.at[send_upper].add(back_upper).at[send_lower].add(back_lower)  27.2 us
    dot_general x12, matrix products, matmul(): return jnp.dot(a, b, preferred_element_type=jnp.float32)  19.3 us
  transfers between devices with their start and end apart: 6, of which 2 were waited for; matrix products, arithmetic and copies ran while one was open for 10% of the time, Pallas kernels for 0%

commit v1 on v0

--- a/solution.py
+++ b/solution.py
@@ -4,6 +4,11 @@
 from jax.sharding import PartitionSpec as P
 
 DEGREE = 16
+
+
+def name_leaves_for(buf):
+    far_arr = lax.all_gather(buf, axis_name="sky")
+    return jnp.sum(far_arr, 0)
 
 
 def passed_along(array, axis, by):
@@ -117,7 +122,7 @@
     used = terms.shape[0]
     chunk = -(-used // (groups * 8)) * 8
     terms = jnp.pad(terms, ((0, chunk * groups - used), (0, 0)))
-    terms = lax.psum(terms, "sky")
+    terms = name_leaves_for(terms)
     mine = lax.dynamic_slice_in_dim(local, start, share, 0) + d_node + to_recv
     local = lax.dynamic_update_slice_in_dim(local, mine, start, 0)
     summed = lax.psum(jnp.concatenate([local, terms], axis=0), "edge")

time: 693 us -> 470 us (0.68)
  waiting for transfers between devices: 474 us -> 245 us
    psum x1 -> x0, waiting for transfers between devices: 246 us -> none  [shards(): terms = lax.psum(terms, 'sky')]
    ppermute x4, waiting for transfers between devices: 0.01 us -> 12.4 us  [passed_along(): lax.ppermute(array, axis, [(i, (i + by) % size) for i in range(size)])]
  transfers between devices with their start and end apart: 6 -> 6, of which waited for: 2 -> 3; matrix products, arithmetic and copies ran while one was open for 10% -> 25% of each run, Pallas kernels for 0% -> 0%
where the time goes in v1:
time: 470 us; the launch traced here: 468 us
  waiting for transfers between devices  245 us (52%)
  other arithmetic  103 us (22%)
  local copies, waits for them, and re-layouts  66.8 us (14%)
  matrix products  30.2 us (6%)
  between operations  14.3 us (3%)
  starting transfers between devices  8.31 us (2%)
    psum x1, waiting for transfers between devices, shards(): summed = lax.psum(jnp.concatenate([local, terms], axis=0), 'edge')  231 us
    scatter-add x1, other arithmetic, shards(): jax.ops.segment_sum(matmul(d_pre, w_send.T), senders, num_segments=nodes...  46.5 us
    gather x1, local copies, waits for them, and re-layouts, shards(): sender_rows = jnp.take(all_rows, senders, axis=0)  32.5 us
    scatter-add x2, other arithmetic, shards(): local = local.at[send_upper].add(back_upper).at[send_lower].add(back_lower)  26.8 us
    dot_general x12, matrix products, matmul(): return jnp.dot(a, b, preferred_element_type=jnp.float32)  20.2 us
    ppermute x4, waiting for transfers between devices, passed_along(): lax.ppermute(array, axis, [(i, (i + by) % size) for i in range(size)])  12.4 us
    dot_general x6, matrix products, outer_sum(): return jnp.einsum('ef,eg->fg', a, b, preferred_element_type=jnp.float32)  9.72 us
  transfers between devices with their start and end apart: 6, of which 3 were waited for; matrix products, arithmetic and copies ran while one was open for 25% of the time, Pallas kernels for 0%

profile of v1, /device:TPU:1, one launch (start us, length us, event | category | flops | bytes accessed | tf_op | source)
XLA Modules:
  0.0 467.8 jit_solution(6756561519701497759)
XLA Ops:
  7.2 0.8 compare_and_fusion.1
  8.8 9.2 %gather_fusion.2 = bf16[2048,128]{1,0:T(8,128)(2,1)} fusion(bf16[4096,128]{1,0:T(8,128)(2,1)} %param.20, s32[2048]{0:T(1024)S(1)} %get-tuple-element.9), kind=kCustom, calls=%fused_computation.1.clone | custom fusion | bytes 1056768 | tf_op jit(solution)/shard_map/jit(_take)/gather | solution.py:60
  17.9 2.2 broadcast_select_fusion.3
  20.1 3.2 collective-permute-start.1
  23.9 8.1 %gather_fusion.1 = bf16[2048,128]{1,0:T(8,128)(2,1)} fusion(bf16[4096,128]{1,0:T(8,128)(2,1)S(1)} %copy-done.1, s32[2048]{0:T(1024)S(1)} %get-tuple-element.11), kind=kCustom, calls=%fused_computation.clone | custom fusion | bytes 1056768 | tf_op jit(solution)/shard_map/jit(_take)/gather | solution.py:59
  32.0 2.2 broadcast_select_fusion.4
  34.4 1.1 fusion.7
  35.5 1.8 convert_reduce_fusion.1
  37.2 1.8 fusion.17
  39.0 0.8 fusion.22
  39.8 0.9 fusion.9
  40.8 0.8 dynamic_slice.18
  41.5 1.4 fusion.30
  42.9 0.8 fusion.15
  43.8 0.8 compare_and_fusion
  44.5 1.7 reshape.64
  46.2 3.5 fusion.3
  49.9 1.8 fusion.16
  51.7 2.7 pad_maximum_fusion.1
  54.4 32.5 %gather_fusion = bf16[8192,128]{1,0:T(8,128)(2,1)} fusion(bf16[8192,128]{1,0:T(8,128)(2,1)} %pad_maximum_fusion.1, s32[8192]{0:T(1024)} %fusion.30), kind=kCustom, calls=%fused_computation.2 | custom fusion | bytes 4227072 | tf_op jit(solution)/shard_map/jit(_take)/gather | solution.py:73
  87.2 1.3 copy-done.5
  88.5 2.7 convolution_add_fusion.1
  92.0 0.9 copy-done.6
  92.8 1.9 fusion.6
  94.8 2.3 bitcast_reduce_fusion
  97.1 2.6 fusion.14
  99.7 1.1 convert_reduce_fusion
  100.8 0.8 convolution_bitcast_fusion
  101.9 2.6 concatenate.10
  104.4 0.8 pad.4
  105.6 4.2 fusion.44
  109.8 46.5 %scatter_custom_fusion = f32[8192,128]{1,0:T(8,128)} fusion(s32[8192]{0:T(1024)} %param.25, f32[8192,128]{1,0:T(8,128)} %fusion.44, f32[]{:T(128)} %constant.10.clone.1), kind=kCustom, calls=%fused_computation.22 | custom fusion | flops 1048576 | bytes 4194816 | tf_op jit(solution)/shard_map/scatter-add | solution.py:93
  156.3 2.6 convert.9
  158.9 0.9 fusion.43
  159.8 4.8 %collective-permute-start.2 = (bf16[2048,128]{1,0:T(8,128)(2,1)S(1)}, bf16[2048,128]{1,0:T(8,128)(2,1)S(1)}, u32[]{:S(2)}, u32[]{:S(2)}) collective-permute-start(bf16[2048,128]{1,0:T(8,128)(2,1)S(1)} %get-tuple-element.7), channel_id=1, source_target_pairs={{0,248},{8,0},{16,8},{24,16},{32,24},{40,32},{48,40},{56,48},{64,5... | collective-permute-start | bytes 1572872 | tf_op jit(solution)/shard_map/ppermute | solution.py:16
  164.6 1.5 slice.41
  166.1 0.9 copy-done.3
  167.7 12.4 %collective-permute-done.2 = bf16[2048,128]{1,0:T(8,128)(2,1)S(1)} collective-permute-done((bf16[2048,128]{1,0:T(8,128)(2,1)S(1)}, bf16[2048,128]{1,0:T(8,128)(2,1)S(1)}, u32[]{:S(2)}, u32[]{:S(2)}) %collective-permute-start.2) | collective-permute-done | bytes 524320 | tf_op jit(solution)/shard_map/ppermute | solution.py:16
  180.2 13.4 %scatter_custom_fusion.1 = f32[4096,128]{1,0:T(8,128)} fusion(f32[4096,128]{1,0:T(8,128)} %slice.41, s32[2048]{0:T(1024)} %get-tuple-element.10, bf16[2048,128]{1,0:T(8,128)(2,1)S(1)} %collective-permute-done.2), kind=kCustom, calls=%fused_computation.37 | custom fusion | flops 524288 | bytes 2621440 | tf_op jit(solution)/shard_map/scatter-add | solution.py:99
  193.6 13.3 %scatter_custom_fusion.2 = f32[4096,128]{1,0:T(8,128)} fusion(f32[4096,128]{1,0:T(8,128)} %scatter_custom_fusion.1, s32[2048]{0:T(1024)S(1)} %get-tuple-element.8, bf16[2048,128]{1,0:T(8,128)(2,1)S(1)} %collective-permute-done.3), kind=kCustom, calls=%fused_computation.35 | custom fusion | flops 524288 | bytes 2621440 | tf_op jit(solution)/shard_map/scatter-add | solution.py:99
  207.0 1.9 add_dynamic-update-slice_fusion
  208.8 1.2 all-gather.3.cloned.1.call-done
  210.1 6.2 %reduce_sum.49 = f32[960,128]{1,0:T(8,128)S(1)} reduce(f32[32,960,128]{2,1,0:T(8,128)} %bitcast.45, f32[]{:T(128)} %constant.10.clone.1), dimensions={0}, to_apply=%region_7.9 | reduce | flops 3809280 | bytes 16220164 | tf_op jit(solution)/shard_map/reduce_sum | solution.py:11
  216.3 3.2 pad_maximum_fusion
  220.3 3.6 convolution_convert_fusion
  223.9 231.3 %all-reduce.3.cloned.1.call-done = f32[5056,128]{1,0:T(8,128)} async-done(((f32[5056,128]{1,0:T(8,128)}), f32[5056,128]{1,0:T(8,128)}) %all-reduce.3.cloned.1.call-update) | async-done | bytes 2588688 | tf_op jit(solution)/shard_map/psum | solution.py:128
  455.3 1.1 slice_multiply_fusion
  458.3 2.7 slice.51
  (68 shorter events, 6.7 us)
Async XLA Ops:
  7.2 84.0 %copy-start = (bf16[8192,128]{1,0:T(8,128)(2,1)S(1)}, bf16[8192,128]{1,0:T(8,128)(2,1)}, u32[]{:S(2)}) copy-start(bf16[8192,128]{1,0:T(8,128)(2,1)} %param.23) | copy-start | bytes 6291460
  7.2 202.9 %all-gather.3.cloned.1.call-start = ((), (), s32[]{:S(2)}) async-start(), calls=%async_computation.1 | async-start | bytes 16220160 | tf_op jit(solution)/shard_map/all_gather | solution.py:10
  8.8 14.5 %copy-start.17 = (s32[2048]{0:T(1024)S(1)}, s32[2048]{0:T(1024)}, u32[]{:S(2)}) copy-start(s32[2048]{0:T(1024)} %param.28) | copy-start | bytes 24580
  8.8 15.2 %copy-start.1 = (bf16[4096,128]{1,0:T(8,128)(2,1)S(1)}, bf16[4096,128]{1,0:T(8,128)(2,1)}, u32[]{:S(2)}) copy-start(bf16[4096,128]{1,0:T(8,128)(2,1)} %param.20) | copy-start | bytes 3145732
  20.1 31.6 %collective-permute-start.1 = (bf16[2048,128]{1,0:T(8,128)(2,1)}, bf16[2048,128]{1,0:T(8,128)(2,1)}, u32[]{:S(2)}, u32[]{:S(2)}) collective-permute-start(bf16[2048,128]{1,0:T(8,128)(2,1)} %broadcast_select_fusion.3), channel_id=1, source_target_pairs={{0,248},{8,0},{16,8},{24,16},{32,24},{40,32},{48,40},{56,48},{64,5... | collective-permute-start | bytes 1572872 | tf_op jit(solution)/shard_map/ppermute | solution.py:16
  23.9 10.3 %copy-start.14 = (bf16[128,128]{1,0:T(8,128)(2,1)S(1)}, bf16[128,128]{1,0:T(8,128)(2,1)}, u32[]{:S(2)}) copy-start(bf16[128,128]{1,0:T(8,128)(2,1)} %param.34) | copy-start | bytes 98308
  23.9 10.4 %copy-start.16 = (bf16[128,128]{1,0:T(8,128)(2,1)S(1)}, bf16[128,128]{1,0:T(8,128)(2,1)}, u32[]{:S(2)}) copy-start(bf16[128,128]{1,0:T(8,128)(2,1)} %param.35) | copy-start | bytes 98308
  23.9 10.4 %copy-start.22 = (f32[128]{0:T(128)S(1)}, f32[128]{0:T(128)}, u32[]{:S(2)}) copy-start(f32[128]{0:T(128)} %param.37) | copy-start | bytes 1540
  32.0 3.5 copy-start.23
  34.2 17.6 %collective-permute-start = (bf16[2048,128]{1,0:T(8,128)(2,1)}, bf16[2048,128]{1,0:T(8,128)(2,1)}, u32[]{:S(2)}, u32[]{:S(2)}) collective-permute-start(bf16[2048,128]{1,0:T(8,128)(2,1)} %broadcast_select_fusion.4), channel_id=1, source_target_pairs={{0,8},{8,16},{16,24},{24,32},{32,40},{40,48},{48,56},{56,64},{64,7... | collective-permute-start | bytes 1572872 | tf_op jit(solution)/shard_map/ppermute | solution.py:16
  35.5 3.5 copy-start.9
  46.2 3.5 copy-start.18
  46.2 3.7 copy-start.10
  86.9 1.6 copy-start.5
  86.9 1.6 copy-start.11
  88.5 2.7 copy-start.12
  88.5 2.7 copy-start.20
  91.2 1.6 copy-start.6
  92.8 1.9 copy-start.24
  97.1 3.7 copy-start.2
  100.8 1.1 copy-start.7
  100.8 1.1 copy-start.8
  100.8 1.1 copy-start.21
  105.3 350.0 %all-reduce.3.cloned.1.call-start = ((), (), s32[]{:S(2)}) async-start(), calls=%async_computation | async-start | bytes 5177344 | tf_op jit(solution)/shard_map/psum | solution.py:128
  156.3 8.3 %copy-start.4 = (f32[8192,128]{1,0:T(8,128)S(1)}, f32[8192,128]{1,0:T(8,128)}, u32[]{:S(2)}) copy-start(f32[8192,128]{1,0:T(8,128)} %scatter_custom_fusion) | copy-start | bytes 12582916
  159.8 20.4 %collective-permute-start.2 = (bf16[2048,128]{1,0:T(8,128)(2,1)S(1)}, bf16[2048,128]{1,0:T(8,128)(2,1)S(1)}, u32[]{:S(2)}, u32[]{:S(2)}) collective-permute-start(bf16[2048,128]{1,0:T(8,128)(2,1)S(1)} %get-tuple-element.7), channel_id=1, source_target_pairs={{0,248},{8,0},{16,8},{24,16},{32,24},{40,32},{48,40},{56,48},{64,5... | collective-permute-start | bytes 1572872 | tf_op jit(solution)/shard_map/ppermute | solution.py:16
  164.6 2.4 copy-start.3
  164.6 2.4 copy-start.19
  164.6 29.0 %collective-permute-start.3 = (bf16[2048,128]{1,0:T(8,128)(2,1)}, bf16[2048,128]{1,0:T(8,128)(2,1)S(1)}, u32[]{:S(2)}, u32[]{:S(2)}) collective-permute-start(bf16[2048,128]{1,0:T(8,128)(2,1)} %get-tuple-element.6), channel_id=1, source_target_pairs={{0,8},{8,16},{16,24},{24,32},{32,40},{40,48},{48,56},{56,64},{64,7... | collective-permute-start | bytes 1572872 | tf_op jit(solution)/shard_map/ppermute | solution.py:16
  193.6 13.4 %copy-start.15 = (bf16[128,128]{1,0:T(8,128)(2,1)S(1)}, bf16[128,128]{1,0:T(8,128)(2,1)}, u32[]{:S(2)}) copy-start(bf16[128,128]{1,0:T(8,128)(2,1)} %param.34) | copy-start | bytes 98308
  219.5 0.8 copy-start.13
Sparse Core Ops, SparseCore 0:
  105.4 104.6 all-gather.2
  219.7 235.5 all-reduce.2
